TPU v7x, 128 devices: a whole 4x4x4 slice. The times are simulated.
128 devices in a mesh: seq: 16 (over y, z), batch: 8 (over x, core).
Axes of the slice: x: 4, y: 4, z: 4, core: 2. Of those that a mesh axis runs over, the one named last changes fastest.
Arguments:
- inputs: bfloat16 [8, 16384, 2048], P('batch', 'seq'), may hold values from -6 to 6
- input_map: bfloat16 [8, 16384, 128], P('batch', 'seq'), may hold values from -0.5 to 0.5
- output_map: bfloat16 [8, 16384, 128], P('batch', 'seq'), may hold values from -0.5 to 0.5
- step_raw: float32 [8, 32, 16384], P('batch', None, 'seq'), may hold values from -4.5 to 4.5
- step_bias: float32 [32], replicated, may hold values from -2 to 0
- decay_rate: float32 [32], replicated, may hold values from 1.5258789e-05 to 0.05
- skip_gain: float32 [32], replicated, may hold values from 0.5 to 1.5
- cotangent: bfloat16 [8, 16384, 2048], P('batch', 'seq'), may hold values from -6 to 6
Outputs:
- grad_inputs: bfloat16 [8, 16384, 2048], P('batch', 'seq')
- grad_input_map: float32 [8, 16384, 128], P('batch', 'seq')
- grad_output_map: float32 [8, 16384, 128], P('batch', 'seq')
- grad_step_raw: float32 [8, 32, 16384], P('batch', None, 'seq')
- grad_params: float32 [2, 32], replicated
- grad_decay_rate: float32 [32], replicated
All inputs are finite; a program needn't handle non-finite values.
Results may differ from a plain program's by a relative error of at most 0.034.
Values sent between devices are 32-bit elements; how exact they have to be, the bound alone decides.
A program may use at most 192 MiB of HBM per device.

v0:
```python
import math
import jax
import jax.numpy as jnp
from jax import lax
from jax.sharding import PartitionSpec as P

GROUP = 256


def entering(array, axis, combine, identity, reverse):
    length, mine = (lax.axis_size(axis), lax.axis_index(axis))
    everything = jax.tree.map(lambda part: lax.all_gather(part, axis), array)
    start = jax.tree.map(
        lambda part, zero: jnp.broadcast_to(jnp.asarray(zero, part.dtype), part.shape),
        array,
        identity,
    )

    def lap(k, before):
        at = length - 1 - k if reverse else k
        reached = at > mine if reverse else at < mine
        new = combine(before, jax.tree.map(lambda part: part[at], everything))
        return jax.tree.map(lambda a, b: jnp.where(reached, a, b), new, before)

    return lax.fori_loop(0, length, lap, start)


def block_step(state, items, skip_gain):
    xc, bc, cc, stepc, logc = items
    width = xc.shape[0]
    cum = jnp.cumsum(logc, axis=1)
    rows = lax.broadcasted_iota(jnp.int32, (width, width), 0)
    cols = lax.broadcasted_iota(jnp.int32, (width, width), 1)
    lower = cols <= rows
    gap = jnp.where(lower[None], cum[:, :, None] - cum[:, None, :], -1e30)
    decay = jnp.exp(gap)
    scores = jnp.einsum("tn,sn->ts", cc, bc, preferred_element_type=jnp.float32)
    weights = (scores[None] * decay * stepc[:, None, :]).astype(jnp.bfloat16)
    inner = jnp.einsum("hts,shp->thp", weights, xc, preferred_element_type=jnp.float32)
    carried = (
        jnp.einsum(
            "tn,hpn->thp", cc, state.astype(jnp.bfloat16), preferred_element_type=jnp.float32
        )
        * jnp.exp(cum).T[:, :, None]
    )
    output = inner + carried + skip_gain[None, :, None] * xc.astype(jnp.float32)
    tail = jnp.exp(cum[:, -1:] - cum) * stepc
    scaled = (xc.astype(jnp.float32) * tail.T[:, :, None]).astype(jnp.bfloat16)
    fresh = jnp.einsum("shp,sn->hpn", scaled, bc, preferred_element_type=jnp.float32)
    new_state = jnp.exp(cum[:, -1])[:, None, None] * state + fresh
    return (new_state, output.astype(jnp.bfloat16))


def scan_forward(xb, bb, cb, raw, step_bias, decay_rate, skip_gain, start_state):
    length, heads, head_size = xb.shape
    states = bb.shape[1]
    blocks = length // GROUP
    step = jax.nn.softplus(raw + step_bias[:, None])
    logd = -decay_rate[:, None] * step
    xs = xb.reshape(blocks, GROUP, heads, head_size)
    bs = bb.reshape(blocks, GROUP, states)
    cs = cb.reshape(blocks, GROUP, states)
    steps = step.reshape(heads, blocks, GROUP).transpose(1, 0, 2)
    logs = logd.reshape(heads, blocks, GROUP).transpose(1, 0, 2)
    body_fn = jax.checkpoint(lambda s, it: block_step(s, it, skip_gain))
    end_state, outs = lax.scan(body_fn, start_state, (xs, bs, cs, steps, logs))
    return (outs.reshape(length, heads, head_size), end_state)


def carry_combine(earlier, later):
    total_e, state_e = earlier
    total_l, state_l = later
    return (total_e + total_l, jnp.exp(total_l)[:, None, None] * state_e + state_l)


def shards(inputs, input_map, output_map, step_raw, step_bias, decay_rate, skip_gain, cotangent):
    length = inputs.shape[1]
    width = inputs.shape[2]
    heads = step_raw.shape[1]
    head_size = width // heads
    states = input_map.shape[2]
    xb = inputs[0].reshape(length, heads, head_size)
    bb = input_map[0]
    cb = output_map[0]
    dyb = cotangent[0].reshape(length, heads, head_size)
    raw = step_raw[0]
    step = jax.nn.softplus(raw + step_bias[:, None])
    logd = -decay_rate[:, None] * step
    cum = jnp.cumsum(logd, axis=1)
    total = cum[:, -1]
    weight_in = jnp.exp(total[:, None] - cum) * step
    scaled_in = (xb.astype(jnp.float32) * weight_in.T[:, :, None]).astype(jnp.bfloat16)
    local_state = jnp.einsum("shp,sn->hpn", scaled_in, bb, preferred_element_type=jnp.float32)
    scaled_grad = dyb.astype(jnp.float32) * jnp.exp(cum).T[:, :, None]
    local_grad = jnp.einsum("thp,tn->hpn", scaled_grad, cb, preferred_element_type=jnp.float32)
    zero_state = jnp.zeros((heads, head_size, states), jnp.float32)
    zero_total = jnp.zeros((heads,), jnp.float32)
    start_state = entering(
        (total, local_state), "seq", carry_combine, (zero_total, zero_state), False
    )[1]
    end_grad = entering((total, local_grad), "seq", carry_combine, (zero_total, zero_state), True)[
        1
    ]

    def local_forward(xv, bv, cv, rv, biasv, ratev, skipv):
        return scan_forward(xv, bv, cv, rv, biasv, ratev, skipv, start_state)

    outputs, pull = jax.vjp(local_forward, xb, bb, cb, raw, step_bias, decay_rate, skip_gain)
    grads = pull((dyb, end_grad))
    params = jnp.stack([grads[4], grads[5], grads[6]])
    total_tokens = length * lax.axis_size("seq") * lax.axis_size("batch")
    summed = lax.psum(params, ("seq", "batch")) * (1.0 / math.sqrt(total_tokens))
    grad_inputs = grads[0].reshape(length, width)[None]
    pair = jnp.stack([summed[0], summed[2]])
    return (
        grad_inputs,
        grads[1].astype(jnp.float32)[None],
        grads[2].astype(jnp.float32)[None],
        grads[3][None],
        pair,
        summed[1],
    )


def solution(mesh):
    in_specs = (
        P("batch", "seq", None),
        P("batch", "seq", None),
        P("batch", "seq", None),
        P("batch", None, "seq"),
        P(),
        P(),
        P(),
        P("batch", "seq", None),
    )
    out_specs = (
        P("batch", "seq", None),
        P("batch", "seq", None),
        P("batch", "seq", None),
        P("batch", None, "seq"),
        P(),
        P(),
    )
    return jax.shard_map(shards, mesh=mesh, in_specs=in_specs, out_specs=out_specs, check_vma=False)
```

profile of v0, /device:TPU:1, one launch (start us, length us, event | category | flops | bytes accessed | tf_op | source)
XLA Modules:
  0.0 635.8 jit_solution(4650788162293645006)
XLA Ops:
  9.6 9.0 %reduce-window.64 = f32[32,8,128]{2,1,0:T(8,128)S(1)} reduce-window(f32[32,8,128]{2,1,0:T(8,128)S(1)} %fusion.79, f32[]{:T(128)} %constant.177.clone.1), window={size=1x1x128 pad=0_0x0_0x127_0}, to_apply=%region_0.1 | reduce-window | flops 4161536 | bytes 262148 | tf_op jit(solution)/shard_map/reduce-window.6
  20.4 6.4 %copy.157 = bf16[1,1024,2048]{1,2,0:T(8,128)(2,1)} copy(bf16[1,1024,2048]{2,1,0:T(8,128)(2,1)} %param.16) | data formatting | bytes 8388608 | tf_op args[0]
  26.8 3.4 fusion.74
  30.2 3.2 fusion.75
  33.4 6.4 %copy.156 = bf16[1,1024,2048]{1,2,0:T(8,128)(2,1)} copy(bf16[1,1024,2048]{2,1,0:T(8,128)(2,1)} %param.23) | data formatting | bytes 8388608 | tf_op args[7]
  39.9 3.4 bitcast_multiply_fusion.5
  43.2 3.2 fusion.77
  46.6 8.0 %reshape_reshape_squeeze.6 = bf16[4,256,32,64]{1,0,3,2:T(4,128)(2,1)} reshape(bf16[1,1024,2048]{1,2,0:T(8,128)(2,1)} %copy.157) | data formatting | bytes 8388608 | tf_op jit(solution)/shard_map/jvp()/reshape;reshape;squeeze | solution.py:60
  54.6 12.9 %reshape.416 = bf16[4,256,32,64]{3,2,1,0:T(8,128)(2,1)} reshape(bf16[1,1024,2048]{2,1,0:T(8,128)(2,1)} %param.23) | data formatting | bytes 8388608 | tf_op jit(solution)/shard_map/transpose(jvp())/reshape;reshape;squeeze | solution.py:67
  69.0 36.4 %all-reduce.2 = f32[512]{0:T(512)S(1)} all-reduce(f32[512]{0:T(512)S(1)} %dynamic-update-slice), channel_id=2, replica_groups=mesh['seq'=16,'batch'=8] {'seq'}, use_global_device_ids=true, to_apply=%add.2 | all-reduce | flops 512 | bytes 4096
  107.1 4.9 copy.160
  112.0 10.4 %copy.167 = bf16[4,256,32,64]{1,3,2,0:T(8,128)(2,1)} copy(bf16[4,256,32,64]{3,2,1,0:T(8,128)(2,1)} %reshape.416) | data formatting | bytes 8388608
  122.4 26.4 %all-gather.8.cloned.1.call-done = f32[512,64,128]{2,1,0:T(8,128)} async-done(((f32[32,64,128]{2,1,0:T(8,128)}), f32[512,64,128]{2,1,0:T(8,128)}) %all-gather.8.cloned.1.call-update) | async-done | bytes 16777232 | tf_op jit(solution)/shard_map/all_gather | solution.py:12
  148.8 24.5 %while.71 = (s32[]{:T(128)}, f32[32,64,128]{2,1,0:T(8,128)S(1)}, s32[]{:T(128)}, f32[16,32]{1,0:T(8,128)S(1)}, f32[16,32,64,128]{3,2,1,0:T(8,128)}, /*index=5*/s32[]{:T(128)}, s32[]{:T(128)}) while((s32[]{:T(128)}, f32[32,64,128]{2,1,0:T(8,128)S(1)}, s32[]{:T(128)}, f32[16,32]{1,0:T(8,128)S(1)}, f32[16,32,64,128]{3,2,1,0:T(8,128)}, ...), condition=%wide.region_5.6_spmd.clone, body=%wide.region_4.5_spmd.clone.sunk | while | flops 1048580 | bytes 3146225 | solution.py:25
  173.3 88.7 %all-gather.6.cloned.1.call-done = f32[512,64,128]{2,1,0:T(8,128)} async-done(((f32[32,64,128]{2,1,0:T(8,128)}), f32[512,64,128]{2,1,0:T(8,128)}) %all-gather.6.cloned.1.call-update) | async-done | bytes 16777232 | tf_op jit(solution)/shard_map/all_gather | solution.py:12
  261.9 24.2 %while.70 = (s32[]{:T(128)}, f32[32,64,128]{2,1,0:T(8,128)S(1)}, s32[]{:T(128)}, f32[16,32]{1,0:T(8,128)S(1)}, f32[16,32,64,128]{3,2,1,0:T(8,128)}, /*index=5*/s32[]{:T(128)}, s32[]{:T(128)}, s32[]{:T(128)}, s32[]{:T(128)}) while((s32[]{:T(128)}, f32[32,64,128]{2,1,0:T(8,128)S(1)}, s32[]{:T(128)}, f32[16,32]{1,0:T(8,128)S(1)}, ...), condition=%wide.region_3.4_spmd.clone, body=%wide.region_2.3_spmd.clone.sunk | while | flops 1048584 | bytes 3146287 | solution.py:25
  286.2 23.5 %while.69 = (s32[]{:T(128)}, f32[32,64,128]{2,1,0:T(8,128)S(1)}, f32[4,32,64,128]{3,2,1,0:T(8,128)}, f32[4,32,256]{2,1,0:T(8,128)}, bf16[4,256,32,64]{1,3,2,0:T(...) while((s32[]{:T(128)}, f32[32,64,128]{2,1,0:T(8,128)S(1)}, ...), condition=%wide.region_9.10_spmd, body=%wide.region_6.9_spmd.sunk | while | flops 137388128 | bytes 5836793 | solution.py:66
  312.5 2.5 broadcast_in_dim.122
  315.0 217.0 %while.72 = (s32[]{:T(128)}, f32[32]{0:T(128)S(1)}, f32[32,64,128]{2,1,0:T(8,128)S(1)}, bf16[4,256,32,64]{1,3,2,0:T(8,128)(2,1)}, bf16[4,256,128]{2,1,0:T(8,128)...) while((s32[]{:T(128)}, f32[32]{0:T(128)S(1)}, ...), condition=%wide.region_24.25_spmd.clone, body=%wide.region_10.0_spmd.clone.sunk | while | flops 1320558848 | bytes 38805324 | solution.py:66
  319.6 2.7 dynamic-slice_bitcast_fusion.11
  327.6 8.2 %fusion.164 = (f32[32,256]{1,0:T(8,128)}, f32[32,256]{1,0:T(8,128)}, f32[32,256]{1,0:T(8,128)}, bf16[256,256]{1,0:T(8,128)(2,1)S(1)}) fusion(f32[32,256]{1,0:T(8,128)} %copy.233, f32[32,256]{1,0:T(8,128)} %copy_bitcast_fusion.10, f32[256,256]{1,0:T(8,128)S(1)} %fusion.163, pred[256,256]{1,0:T(8,128)(4,1)} %iota_compare_fusion.2, ...), kind=kOutput, calls=%fused_computation.36.clone.1 | convolution fusion | flops 299802624 | bytes 2719744 | tf_op jit(solution)/shard_map/transpose(jvp())/while/body/eval_jaxpr/checkpoint/hts,shp->thp/dot_general | solution.py:39
  341.9 3.6 fusion.161
  348.0 2.0 fusion.167
  354.7 2.4 fusion.172
  357.8 2.5 reduce-window.80
  364.6 4.6 fusion.170
  373.9 2.7 dynamic-slice_bitcast_fusion.11
  381.9 8.2 %fusion.164 = (f32[32,256]{1,0:T(8,128)}, f32[32,256]{1,0:T(8,128)}, f32[32,256]{1,0:T(8,128)}, bf16[256,256]{1,0:T(8,128)(2,1)S(1)}) fusion(f32[32,256]{1,0:T(8,128)} %copy.233, f32[32,256]{1,0:T(8,128)} %copy_bitcast_fusion.10, f32[256,256]{1,0:T(8,128)S(1)} %fusion.163, pred[256,256]{1,0:T(8,128)(4,1)} %iota_compare_fusion.2, ...), kind=kOutput, calls=%fused_computation.36.clone.1 | convolution fusion | flops 299802624 | bytes 2719744 | tf_op jit(solution)/shard_map/transpose(jvp())/while/body/eval_jaxpr/checkpoint/hts,shp->thp/dot_general | solution.py:39
  396.2 3.6 fusion.161
  402.2 2.0 fusion.167
  408.9 2.4 fusion.172
  412.0 2.5 reduce-window.80
  418.8 4.6 fusion.170
  428.1 2.7 dynamic-slice_bitcast_fusion.11
  436.1 8.2 %fusion.164 = (f32[32,256]{1,0:T(8,128)}, f32[32,256]{1,0:T(8,128)}, f32[32,256]{1,0:T(8,128)}, bf16[256,256]{1,0:T(8,128)(2,1)S(1)}) fusion(f32[32,256]{1,0:T(8,128)} %copy.233, f32[32,256]{1,0:T(8,128)} %copy_bitcast_fusion.10, f32[256,256]{1,0:T(8,128)S(1)} %fusion.163, pred[256,256]{1,0:T(8,128)(4,1)} %iota_compare_fusion.2, ...), kind=kOutput, calls=%fused_computation.36.clone.1 | convolution fusion | flops 299802624 | bytes 2719744 | tf_op jit(solution)/shard_map/transpose(jvp())/while/body/eval_jaxpr/checkpoint/hts,shp->thp/dot_general | solution.py:39
  450.4 3.6 fusion.161
  463.2 2.4 fusion.172
  466.3 2.5 reduce-window.80
  473.1 4.6 fusion.170
  482.4 2.7 dynamic-slice_bitcast_fusion.11
  490.4 8.2 %fusion.164 = (f32[32,256]{1,0:T(8,128)}, f32[32,256]{1,0:T(8,128)}, f32[32,256]{1,0:T(8,128)}, bf16[256,256]{1,0:T(8,128)(2,1)S(1)}) fusion(f32[32,256]{1,0:T(8,128)} %copy.233, f32[32,256]{1,0:T(8,128)} %copy_bitcast_fusion.10, f32[256,256]{1,0:T(8,128)S(1)} %fusion.163, pred[256,256]{1,0:T(8,128)(4,1)} %iota_compare_fusion.2, ...), kind=kOutput, calls=%fused_computation.36.clone.1 | convolution fusion | flops 299802624 | bytes 2719744 | tf_op jit(solution)/shard_map/transpose(jvp())/while/body/eval_jaxpr/checkpoint/hts,shp->thp/dot_general | solution.py:39
  504.7 3.6 fusion.161
  517.4 2.4 fusion.172
  520.5 2.5 reduce-window.80
  527.3 4.6 fusion.170
  533.9 64.8 %psum.7 = f32[3,32]{1,0:T(4,128)S(1)} all-reduce(f32[3,32]{1,0:T(4,128)S(1)} %pad_maximum_fusion), channel_id=1, replica_groups=mesh['seq'=16,'batch'=8] {'seq','batch'}, use_global_device_ids=true, to_apply=%region_27.28 | all-reduce | flops 96 | bytes 768 | tf_op jit(solution)/shard_map/psum | solution.py:112
  601.2 12.9 %copy.174 = bf16[4,256,32,64]{3,2,1,0:T(8,128)(2,1)} copy(bf16[4,256,32,64]{1,3,2,0:T(8,128)(2,1)} %get-tuple-element.598) | data formatting | bytes 8388608
  614.1 12.4 %reshape.417 = bf16[1,1024,2048]{2,1,0:T(8,128)(2,1)} reshape(bf16[4,256,32,64]{3,2,1,0:T(8,128)(2,1)} %copy.174) | data formatting | bytes 8388608
  (403 shorter events, 203.9 us)
Async XLA Ops:
  7.2 141.7 %all-gather.8.cloned.1.call-start = ((), (), s32[]{:S(2)}) async-start(), calls=%async_computation.1 | async-start | bytes 17825792 | tf_op jit(solution)/shard_map/all_gather | solution.py:12
  7.9 97.6 %copy-start.13 = (f32[32]{0:T(128)}, f32[32]{0:T(128)S(1)}, u32[]{:S(2)}) copy-start(f32[32]{0:T(128)S(1)} %neg.50) | copy-start | bytes 388
  33.4 228.6 %all-gather.6.cloned.1.call-start = ((), (), s32[]{:S(2)}) async-start(), calls=%async_computation | async-start | bytes 17825792 | tf_op jit(solution)/shard_map/all_gather | solution.py:12
  43.2 3.3 copy-start.5
  46.6 58.9 %copy-start.7 = (f32[32,4,256]{2,1,0:T(4,128)}, f32[32,4,256]{2,1,0:T(4,128)S(1)}, u32[]{:S(2)}) copy-start(f32[32,4,256]{2,1,0:T(4,128)S(1)} %squeeze.124) | copy-start | bytes 393220
  54.6 12.9 %copy-start.16 = (u32[128]{0:T(128)S(1)}, u32[128]{0:T(128)}, u32[]{:S(2)}) copy-start(u32[128]{0:T(128)} %constant.194) | copy-start | bytes 1540
  54.6 50.9 %copy-start.10 = (f32[32]{0:T(128)S(1)}, f32[32]{0:T(128)}, u32[]{:S(2)}) copy-start(f32[32]{0:T(128)} %param.20) | copy-start | bytes 388
  327.6 8.2 %copy-start.3 = (f32[256,256]{1,0:T(8,128)}, f32[256,256]{1,0:T(8,128)S(1)}, u32[]{:S(2)}) copy-start(f32[256,256]{1,0:T(8,128)S(1)} %fusion.163) | copy-start | bytes 786436 | tf_op jit(solution)/shard_map/transpose(jvp())/while
  345.5 18.4 %copy-start.12 = (f32[32]{0:T(128)S(1)}, f32[32]{0:T(128)}, u32[]{:S(2)}) copy-start(f32[32]{0:T(128)} %fusion.168) | copy-start | bytes 388 | tf_op jit(solution)/shard_map/transpose(jvp())/while
  350.0 7.1 %copy-start.2 = (f32[1,32,256]{1,2,0:T(8,128)S(1)}, f32[1,32,256]{1,2,0:T(8,128)}, u32[]{:S(2)}) copy-start(f32[1,32,256]{1,2,0:T(8,128)} %get-tuple-element.1214) | copy-start | bytes 98308 | tf_op jit(solution)/shard_map/transpose(jvp())/while
  350.0 7.7 %copy-start.1 = (f32[32,256]{0,1:T(8,128)S(1)}, f32[32,256]{0,1:T(8,128)}, u32[]{:S(2)}) copy-start(f32[32,256]{0,1:T(8,128)} %get-tuple-element.1215) | copy-start | bytes 98308 | tf_op jit(solution)/shard_map/transpose(jvp())/while
  351.0 13.6 %copy-start.4 = (f32[32,256]{1,0:T(8,128)S(1)}, f32[32,256]{1,0:T(8,128)}, u32[]{:S(2)}) copy-start(f32[32,256]{1,0:T(8,128)} %copy_bitcast_fusion.10) | copy-start | bytes 98308 | tf_op jit(solution)/shard_map/transpose(jvp())/while
  351.0 13.6 %copy-start.15 = (f32[32]{0:T(128)S(1)}, f32[32]{0:T(128)}, u32[]{:S(2)}) copy-start(f32[32]{0:T(128)} %get-tuple-element.1211) | copy-start | bytes 388 | tf_op jit(solution)/shard_map/transpose(jvp())/while
  353.0 11.6 %copy-start = (bf16[256,32,64]{0,2,1:T(8,128)(2,1)S(1)}, bf16[256,32,64]{0,2,1:T(8,128)(2,1)}, u32[]{:S(2)}) copy-start(bf16[256,32,64]{0,2,1:T(8,128)(2,1)} %get-tuple-element.1210) | copy-start | bytes 3145732 | tf_op jit(solution)/shard_map/transpose(jvp())/while
  381.9 8.2 %copy-start.3 = (f32[256,256]{1,0:T(8,128)}, f32[256,256]{1,0:T(8,128)S(1)}, u32[]{:S(2)}) copy-start(f32[256,256]{1,0:T(8,128)S(1)} %fusion.163) | copy-start | bytes 786436 | tf_op jit(solution)/shard_map/transpose(jvp())/while
  399.8 18.4 %copy-start.12 = (f32[32]{0:T(128)S(1)}, f32[32]{0:T(128)}, u32[]{:S(2)}) copy-start(f32[32]{0:T(128)} %fusion.168) | copy-start | bytes 388 | tf_op jit(solution)/shard_map/transpose(jvp())/while
  404.2 7.1 %copy-start.2 = (f32[1,32,256]{1,2,0:T(8,128)S(1)}, f32[1,32,256]{1,2,0:T(8,128)}, u32[]{:S(2)}) copy-start(f32[1,32,256]{1,2,0:T(8,128)} %get-tuple-element.1214) | copy-start | bytes 98308 | tf_op jit(solution)/shard_map/transpose(jvp())/while
  404.2 7.7 %copy-start.1 = (f32[32,256]{0,1:T(8,128)S(1)}, f32[32,256]{0,1:T(8,128)}, u32[]{:S(2)}) copy-start(f32[32,256]{0,1:T(8,128)} %get-tuple-element.1215) | copy-start | bytes 98308 | tf_op jit(solution)/shard_map/transpose(jvp())/while
  405.2 13.6 %copy-start.4 = (f32[32,256]{1,0:T(8,128)S(1)}, f32[32,256]{1,0:T(8,128)}, u32[]{:S(2)}) copy-start(f32[32,256]{1,0:T(8,128)} %copy_bitcast_fusion.10) | copy-start | bytes 98308 | tf_op jit(solution)/shard_map/transpose(jvp())/while
  405.2 13.6 %copy-start.15 = (f32[32]{0:T(128)S(1)}, f32[32]{0:T(128)}, u32[]{:S(2)}) copy-start(f32[32]{0:T(128)} %get-tuple-element.1211) | copy-start | bytes 388 | tf_op jit(solution)/shard_map/transpose(jvp())/while
  407.2 11.6 %copy-start = (bf16[256,32,64]{0,2,1:T(8,128)(2,1)S(1)}, bf16[256,32,64]{0,2,1:T(8,128)(2,1)}, u32[]{:S(2)}) copy-start(bf16[256,32,64]{0,2,1:T(8,128)(2,1)} %get-tuple-element.1210) | copy-start | bytes 3145732 | tf_op jit(solution)/shard_map/transpose(jvp())/while
  436.1 8.2 %copy-start.3 = (f32[256,256]{1,0:T(8,128)}, f32[256,256]{1,0:T(8,128)S(1)}, u32[]{:S(2)}) copy-start(f32[256,256]{1,0:T(8,128)S(1)} %fusion.163) | copy-start | bytes 786436 | tf_op jit(solution)/shard_map/transpose(jvp())/while
  454.0 18.4 %copy-start.12 = (f32[32]{0:T(128)S(1)}, f32[32]{0:T(128)}, u32[]{:S(2)}) copy-start(f32[32]{0:T(128)} %fusion.168) | copy-start | bytes 388 | tf_op jit(solution)/shard_map/transpose(jvp())/while
  458.5 7.1 %copy-start.2 = (f32[1,32,256]{1,2,0:T(8,128)S(1)}, f32[1,32,256]{1,2,0:T(8,128)}, u32[]{:S(2)}) copy-start(f32[1,32,256]{1,2,0:T(8,128)} %get-tuple-element.1214) | copy-start | bytes 98308 | tf_op jit(solution)/shard_map/transpose(jvp())/while
  458.5 7.7 %copy-start.1 = (f32[32,256]{0,1:T(8,128)S(1)}, f32[32,256]{0,1:T(8,128)}, u32[]{:S(2)}) copy-start(f32[32,256]{0,1:T(8,128)} %get-tuple-element.1215) | copy-start | bytes 98308 | tf_op jit(solution)/shard_map/transpose(jvp())/while
  459.5 13.6 %copy-start.4 = (f32[32,256]{1,0:T(8,128)S(1)}, f32[32,256]{1,0:T(8,128)}, u32[]{:S(2)}) copy-start(f32[32,256]{1,0:T(8,128)} %copy_bitcast_fusion.10) | copy-start | bytes 98308 | tf_op jit(solution)/shard_map/transpose(jvp())/while
  459.5 13.6 %copy-start.15 = (f32[32]{0:T(128)S(1)}, f32[32]{0:T(128)}, u32[]{:S(2)}) copy-start(f32[32]{0:T(128)} %get-tuple-element.1211) | copy-start | bytes 388 | tf_op jit(solution)/shard_map/transpose(jvp())/while
  461.5 11.6 %copy-start = (bf16[256,32,64]{0,2,1:T(8,128)(2,1)S(1)}, bf16[256,32,64]{0,2,1:T(8,128)(2,1)}, u32[]{:S(2)}) copy-start(bf16[256,32,64]{0,2,1:T(8,128)(2,1)} %get-tuple-element.1210) | copy-start | bytes 3145732 | tf_op jit(solution)/shard_map/transpose(jvp())/while
  490.4 8.2 %copy-start.3 = (f32[256,256]{1,0:T(8,128)}, f32[256,256]{1,0:T(8,128)S(1)}, u32[]{:S(2)}) copy-start(f32[256,256]{1,0:T(8,128)S(1)} %fusion.163) | copy-start | bytes 786436 | tf_op jit(solution)/shard_map/transpose(jvp())/while
  508.2 18.4 %copy-start.12 = (f32[32]{0:T(128)S(1)}, f32[32]{0:T(128)}, u32[]{:S(2)}) copy-start(f32[32]{0:T(128)} %fusion.168) | copy-start | bytes 388 | tf_op jit(solution)/shard_map/transpose(jvp())/while
  512.7 7.1 %copy-start.2 = (f32[1,32,256]{1,2,0:T(8,128)S(1)}, f32[1,32,256]{1,2,0:T(8,128)}, u32[]{:S(2)}) copy-start(f32[1,32,256]{1,2,0:T(8,128)} %get-tuple-element.1214) | copy-start | bytes 98308 | tf_op jit(solution)/shard_map/transpose(jvp())/while
  512.7 7.7 %copy-start.1 = (f32[32,256]{0,1:T(8,128)S(1)}, f32[32,256]{0,1:T(8,128)}, u32[]{:S(2)}) copy-start(f32[32,256]{0,1:T(8,128)} %get-tuple-element.1215) | copy-start | bytes 98308 | tf_op jit(solution)/shard_map/transpose(jvp())/while
  513.7 13.6 %copy-start.4 = (f32[32,256]{1,0:T(8,128)S(1)}, f32[32,256]{1,0:T(8,128)}, u32[]{:S(2)}) copy-start(f32[32,256]{1,0:T(8,128)} %copy_bitcast_fusion.10) | copy-start | bytes 98308 | tf_op jit(solution)/shard_map/transpose(jvp())/while
  513.7 13.6 %copy-start.15 = (f32[32]{0:T(128)S(1)}, f32[32]{0:T(128)}, u32[]{:S(2)}) copy-start(f32[32]{0:T(128)} %get-tuple-element.1211) | copy-start | bytes 388 | tf_op jit(solution)/shard_map/transpose(jvp())/while
  515.7 11.6 %copy-start = (bf16[256,32,64]{0,2,1:T(8,128)(2,1)S(1)}, bf16[256,32,64]{0,2,1:T(8,128)(2,1)}, u32[]{:S(2)}) copy-start(bf16[256,32,64]{0,2,1:T(8,128)(2,1)} %get-tuple-element.1210) | copy-start | bytes 3145732 | tf_op jit(solution)/shard_map/transpose(jvp())/while
  614.1 13.0 %copy-start.6 = (f32[1,32,1024]{2,1,0:T(8,128)S(1)}, f32[1,32,1024]{2,1,0:T(8,128)}, u32[]{:S(2)}) copy-start(f32[1,32,1024]{2,1,0:T(8,128)} %param.19) | copy-start | bytes 393220
  614.1 13.0 %copy-start.11 = (f32[32]{0:T(128)S(1)}, f32[32]{0:T(128)}, u32[]{:S(2)}) copy-start(f32[32]{0:T(128)} %param.20) | copy-start | bytes 388
  614.1 13.0 %copy-start.14 = (f32[32]{0:T(128)S(1)}, f32[32]{0:T(128)}, u32[]{:S(2)}) copy-start(f32[32]{0:T(128)} %copy-done.13) | copy-start | bytes 388
  614.1 13.8 %copy-start.8 = (bf16[4,256,128]{2,1,0:T(8,128)(2,1)S(1)}, bf16[4,256,128]{2,1,0:T(8,128)(2,1)}, u32[]{:S(2)}) copy-start(bf16[4,256,128]{2,1,0:T(8,128)(2,1)} %get-tuple-element.600) | copy-start | bytes 786436
  614.1 13.8 %copy-start.9 = (bf16[4,256,128]{2,1,0:T(8,128)(2,1)S(1)}, bf16[4,256,128]{2,1,0:T(8,128)(2,1)}, u32[]{:S(2)}) copy-start(bf16[4,256,128]{2,1,0:T(8,128)(2,1)} %get-tuple-element.599) | copy-start | bytes 786436
Sparse Core Ops, SparseCore 0:
  33.5 115.2 all-gather.7
  151.0 110.9 all-gather.5
where the time goes:
time: 643 us; the launch traced here: 636 us
  local copies, waits for them, and re-layouts  189 us (29%)
  waiting for transfers between devices  115 us (18%)
  matrix products  108 us (17%)
  other arithmetic  106 us (16%)
  blocking collectives  101 us (16%)
  between operations  14.9 us (2%)
    all_gather x2, waiting for transfers between devices, entering(): everything = jax.tree.map(lambda part: lax.all_gather(part, axis), array)  115 us
    psum x1, blocking collectives, shards(): lax.psum(params, ('seq', 'batch')) * (1.0 / math.sqrt(total_tokens))  64.8 us
    dot_general x8, matrix products, block_step(): jnp.einsum('hts,shp->thp', weights, xc, preferred_element_type=jnp.float32)  51.3 us
    unnamed x30, local copies, waits for them, and re-layouts  50.4 us
    select_n x32, other arithmetic, lap(): return jax.tree.map(lambda a, b: jnp.where(reached, a, b), new, before)  47.2 us
    unnamed x1, blocking collectives  36.4 us
    dot_general x12, matrix products, block_step(): jnp.einsum('shp,sn->hpn', scaled, bc, preferred_element_type=jnp.float32)  31.1 us
    another operation x39, other arithmetic  27.7 us
  transfers between devices with their start and end apart: 2, of which 2 were waited for; matrix products, arithmetic and copies ran while one was open for 12% of the time, Pallas kernels for 0%

commit v1 on v0

--- a/solution.py
+++ b/solution.py
@@ -5,6 +5,11 @@
 from jax.sharding import PartitionSpec as P
 
 GROUP = 256
+
+
+def leaves_view(vals):
+    left_arr = jnp.sum(lax.all_gather(vals, ("seq", "batch")), 0)
+    return left_arr
 
 
 def entering(array, axis, combine, identity, reverse):
@@ -109,7 +114,7 @@
     grads = pull((dyb, end_grad))
     params = jnp.stack([grads[4], grads[5], grads[6]])
     total_tokens = length * lax.axis_size("seq") * lax.axis_size("batch")
-    summed = lax.psum(params, ("seq", "batch")) * (1.0 / math.sqrt(total_tokens))
+    summed = leaves_view(params) * (1.0 / math.sqrt(total_tokens))
     grad_inputs = grads[0].reshape(length, width)[None]
     pair = jnp.stack([summed[0], summed[2]])
     return (

time: 643 us -> 614 us (0.955)
  blocking collectives: 101 us -> 72.4 us
    psum x1 -> x0, blocking collectives: 64.8 us -> none  [shards(): lax.psum(params, ('seq', 'batch')) * (1.0 / math.sqrt(total_tokens))]
    all_gather x0 -> x1, blocking collectives: none -> 36 us  [leaves_view(): left_arr = jnp.sum(lax.all_gather(vals, ('seq', 'batch')), 0)]
    another operation x40 -> x39, other arithmetic: 27.7 us -> 27.7 us
where the time goes in v1:
time: 614 us; the launch traced here: 607 us
  local copies, waits for them, and re-layouts  189 us (31%)
  waiting for transfers between devices  115 us (19%)
  matrix products  108 us (18%)
  other arithmetic  106 us (17%)
  blocking collectives  72.4 us (12%)
  between operations  14.9 us (2%)
    all_gather x2, waiting for transfers between devices, entering(): everything = jax.tree.map(lambda part: lax.all_gather(part, axis), array)  115 us
    dot_general x8, matrix products, block_step(): jnp.einsum('hts,shp->thp', weights, xc, preferred_element_type=jnp.float32)  51.3 us
    unnamed x30, local copies, waits for them, and re-layouts  50.4 us
    select_n x32, other arithmetic, lap(): return jax.tree.map(lambda a, b: jnp.where(reached, a, b), new, before)  47.2 us
    unnamed x1, blocking collectives  36.4 us
    all_gather x1, blocking collectives, leaves_view(): left_arr = jnp.sum(lax.all_gather(vals, ('seq', 'batch')), 0)  36 us
    dot_general x12, matrix products, block_step(): jnp.einsum('shp,sn->hpn', scaled, bc, preferred_element_type=jnp.float32)  31.1 us
    another operation x39, other arithmetic  27.7 us
  transfers between devices with their start and end apart: 2, of which 2 were waited for; matrix products, arithmetic and copies ran while one was open for 12% of the time, Pallas kernels for 0%

profile of v1, /device:TPU:1, one launch (start us, length us, event | category | flops | bytes accessed | tf_op | source)
XLA Modules:
  0.0 607.2 jit_solution(7455594441476788650)
XLA Ops:
  9.6 9.0 %reduce-window.64 = f32[32,8,128]{2,1,0:T(8,128)S(1)} reduce-window(f32[32,8,128]{2,1,0:T(8,128)S(1)} %fusion.79, f32[]{:T(128)} %constant.177.clone.1), window={size=1x1x128 pad=0_0x0_0x127_0}, to_apply=%region_0.1 | reduce-window | flops 4161536 | bytes 262148 | tf_op jit(solution)/shard_map/reduce-window.6
  20.4 6.4 %copy.157 = bf16[1,1024,2048]{1,2,0:T(8,128)(2,1)} copy(bf16[1,1024,2048]{2,1,0:T(8,128)(2,1)} %param.16) | data formatting | bytes 8388608 | tf_op args[0]
  26.8 3.4 fusion.74
  30.2 3.2 fusion.75
  33.4 6.4 %copy.156 = bf16[1,1024,2048]{1,2,0:T(8,128)(2,1)} copy(bf16[1,1024,2048]{2,1,0:T(8,128)(2,1)} %param.23) | data formatting | bytes 8388608 | tf_op args[7]
  39.9 3.4 bitcast_multiply_fusion.5
  43.2 3.2 fusion.77
  46.6 8.0 %reshape_reshape_squeeze.6 = bf16[4,256,32,64]{1,0,3,2:T(4,128)(2,1)} reshape(bf16[1,1024,2048]{1,2,0:T(8,128)(2,1)} %copy.157) | data formatting | bytes 8388608 | tf_op jit(solution)/shard_map/jvp()/reshape;reshape;squeeze | solution.py:65
  54.6 12.9 %reshape.420 = bf16[4,256,32,64]{3,2,1,0:T(8,128)(2,1)} reshape(bf16[1,1024,2048]{2,1,0:T(8,128)(2,1)} %param.23) | data formatting | bytes 8388608 | tf_op jit(solution)/shard_map/transpose(jvp())/reshape;reshape;squeeze | solution.py:72
  69.0 36.4 %all-reduce.2 = f32[512]{0:T(512)S(1)} all-reduce(f32[512]{0:T(512)S(1)} %dynamic-update-slice), channel_id=2, replica_groups=mesh['seq'=16,'batch'=8] {'seq'}, use_global_device_ids=true, to_apply=%add.2 | all-reduce | flops 512 | bytes 4096
  107.1 4.9 copy.160
  112.0 10.4 %copy.167 = bf16[4,256,32,64]{1,3,2,0:T(8,128)(2,1)} copy(bf16[4,256,32,64]{3,2,1,0:T(8,128)(2,1)} %reshape.420) | data formatting | bytes 8388608
  122.4 26.4 %all-gather.10.cloned.1.call-done = f32[512,64,128]{2,1,0:T(8,128)} async-done(((f32[32,64,128]{2,1,0:T(8,128)}), f32[512,64,128]{2,1,0:T(8,128)}) %all-gather.10.cloned.1.call-update) | async-done | bytes 16777232 | tf_op jit(solution)/shard_map/all_gather | solution.py:17
  148.8 24.5 %while.71 = (s32[]{:T(128)}, f32[32,64,128]{2,1,0:T(8,128)S(1)}, s32[]{:T(128)}, f32[16,32]{1,0:T(8,128)S(1)}, f32[16,32,64,128]{3,2,1,0:T(8,128)}, /*index=5*/s32[]{:T(128)}, s32[]{:T(128)}) while((s32[]{:T(128)}, f32[32,64,128]{2,1,0:T(8,128)S(1)}, s32[]{:T(128)}, f32[16,32]{1,0:T(8,128)S(1)}, f32[16,32,64,128]{3,2,1,0:T(8,128)}, ...), condition=%wide.region_5.6_spmd.clone, body=%wide.region_4.5_spmd.clone.sunk | while | flops 1048580 | bytes 3146225 | solution.py:30
  173.3 88.7 %all-gather.8.cloned.1.call-done = f32[512,64,128]{2,1,0:T(8,128)} async-done(((f32[32,64,128]{2,1,0:T(8,128)}), f32[512,64,128]{2,1,0:T(8,128)}) %all-gather.8.cloned.1.call-update) | async-done | bytes 16777232 | tf_op jit(solution)/shard_map/all_gather | solution.py:17
  261.9 24.2 %while.70 = (s32[]{:T(128)}, f32[32,64,128]{2,1,0:T(8,128)S(1)}, s32[]{:T(128)}, f32[16,32]{1,0:T(8,128)S(1)}, f32[16,32,64,128]{3,2,1,0:T(8,128)}, /*index=5*/s32[]{:T(128)}, s32[]{:T(128)}, s32[]{:T(128)}, s32[]{:T(128)}) while((s32[]{:T(128)}, f32[32,64,128]{2,1,0:T(8,128)S(1)}, s32[]{:T(128)}, f32[16,32]{1,0:T(8,128)S(1)}, ...), condition=%wide.region_3.4_spmd.clone, body=%wide.region_2.3_spmd.clone.sunk | while | flops 1048584 | bytes 3146287 | solution.py:30
  286.2 23.5 %while.69 = (s32[]{:T(128)}, f32[32,64,128]{2,1,0:T(8,128)S(1)}, f32[4,32,64,128]{3,2,1,0:T(8,128)}, f32[4,32,256]{2,1,0:T(8,128)}, bf16[4,256,32,64]{1,3,2,0:T(...) while((s32[]{:T(128)}, f32[32,64,128]{2,1,0:T(8,128)S(1)}, ...), condition=%wide.region_9.10_spmd, body=%wide.region_6.9_spmd.sunk | while | flops 137388128 | bytes 5836793 | solution.py:71
  312.5 2.5 broadcast_in_dim.122
  315.0 217.0 %while.72 = (s32[]{:T(128)}, f32[32]{0:T(128)S(1)}, f32[32,64,128]{2,1,0:T(8,128)S(1)}, bf16[4,256,32,64]{1,3,2,0:T(8,128)(2,1)}, bf16[4,256,128]{2,1,0:T(8,128)...) while((s32[]{:T(128)}, f32[32]{0:T(128)S(1)}, ...), condition=%wide.region_24.25_spmd.clone, body=%wide.region_10.0_spmd.clone.sunk | while | flops 1320558848 | bytes 38805324 | solution.py:71
  319.6 2.7 dynamic-slice_bitcast_fusion.11
  327.6 8.2 %fusion.164 = (f32[32,256]{1,0:T(8,128)}, f32[32,256]{1,0:T(8,128)}, f32[32,256]{1,0:T(8,128)}, bf16[256,256]{1,0:T(8,128)(2,1)S(1)}) fusion(f32[32,256]{1,0:T(8,128)} %copy.234, f32[32,256]{1,0:T(8,128)} %copy_bitcast_fusion.10, f32[256,256]{1,0:T(8,128)S(1)} %fusion.163, pred[256,256]{1,0:T(8,128)(4,1)} %iota_compare_fusion.2, ...), kind=kOutput, calls=%fused_computation.36.clone.1 | convolution fusion | flops 299802624 | bytes 2719744 | tf_op jit(solution)/shard_map/transpose(jvp())/while/body/eval_jaxpr/checkpoint/hts,shp->thp/dot_general | solution.py:44
  341.9 3.6 fusion.161
  348.0 2.0 fusion.167
  354.7 2.4 fusion.172
  357.8 2.5 reduce-window.80
  364.6 4.6 fusion.170
  373.9 2.7 dynamic-slice_bitcast_fusion.11
  381.9 8.2 %fusion.164 = (f32[32,256]{1,0:T(8,128)}, f32[32,256]{1,0:T(8,128)}, f32[32,256]{1,0:T(8,128)}, bf16[256,256]{1,0:T(8,128)(2,1)S(1)}) fusion(f32[32,256]{1,0:T(8,128)} %copy.234, f32[32,256]{1,0:T(8,128)} %copy_bitcast_fusion.10, f32[256,256]{1,0:T(8,128)S(1)} %fusion.163, pred[256,256]{1,0:T(8,128)(4,1)} %iota_compare_fusion.2, ...), kind=kOutput, calls=%fused_computation.36.clone.1 | convolution fusion | flops 299802624 | bytes 2719744 | tf_op jit(solution)/shard_map/transpose(jvp())/while/body/eval_jaxpr/checkpoint/hts,shp->thp/dot_general | solution.py:44
  396.2 3.6 fusion.161
  402.2 2.0 fusion.167
  408.9 2.4 fusion.172
  412.0 2.5 reduce-window.80
  418.8 4.6 fusion.170
  428.1 2.7 dynamic-slice_bitcast_fusion.11
  436.1 8.2 %fusion.164 = (f32[32,256]{1,0:T(8,128)}, f32[32,256]{1,0:T(8,128)}, f32[32,256]{1,0:T(8,128)}, bf16[256,256]{1,0:T(8,128)(2,1)S(1)}) fusion(f32[32,256]{1,0:T(8,128)} %copy.234, f32[32,256]{1,0:T(8,128)} %copy_bitcast_fusion.10, f32[256,256]{1,0:T(8,128)S(1)} %fusion.163, pred[256,256]{1,0:T(8,128)(4,1)} %iota_compare_fusion.2, ...), kind=kOutput, calls=%fused_computation.36.clone.1 | convolution fusion | flops 299802624 | bytes 2719744 | tf_op jit(solution)/shard_map/transpose(jvp())/while/body/eval_jaxpr/checkpoint/hts,shp->thp/dot_general | solution.py:44
  450.4 3.6 fusion.161
  463.2 2.4 fusion.172
  466.3 2.5 reduce-window.80
  473.1 4.6 fusion.170
  482.4 2.7 dynamic-slice_bitcast_fusion.11
  490.4 8.2 %fusion.164 = (f32[32,256]{1,0:T(8,128)}, f32[32,256]{1,0:T(8,128)}, f32[32,256]{1,0:T(8,128)}, bf16[256,256]{1,0:T(8,128)(2,1)S(1)}) fusion(f32[32,256]{1,0:T(8,128)} %copy.234, f32[32,256]{1,0:T(8,128)} %copy_bitcast_fusion.10, f32[256,256]{1,0:T(8,128)S(1)} %fusion.163, pred[256,256]{1,0:T(8,128)(4,1)} %iota_compare_fusion.2, ...), kind=kOutput, calls=%fused_computation.36.clone.1 | convolution fusion | flops 299802624 | bytes 2719744 | tf_op jit(solution)/shard_map/transpose(jvp())/while/body/eval_jaxpr/checkpoint/hts,shp->thp/dot_general | solution.py:44
  504.7 3.6 fusion.161
  517.4 2.4 fusion.172
  520.5 2.5 reduce-window.80
  527.3 4.6 fusion.170
  535.8 36.0 %all-gather.4 = f32[128,3,32]{2,1,0:T(4,128)S(1)} all-gather(f32[1,3,32]{2,1,0:T(4,128)S(1)} %maximum_bitcast_fusion), channel_id=5, replica_groups=mesh['seq'=16,'batch'=8] {'seq','batch'}, dimensions={0}, use_global_device_ids=true | all-gather | bytes 49536 | tf_op jit(solution)/shard_map/all_gather | solution.py:11
  572.5 12.9 %copy.174 = bf16[4,256,32,64]{3,2,1,0:T(8,128)(2,1)} copy(bf16[4,256,32,64]{1,3,2,0:T(8,128)(2,1)} %get-tuple-element.598) | data formatting | bytes 8388608
  585.5 12.4 %reshape.421 = bf16[1,1024,2048]{2,1,0:T(8,128)(2,1)} reshape(bf16[4,256,32,64]{3,2,1,0:T(8,128)(2,1)} %copy.174) | data formatting | bytes 8388608
  (404 shorter events, 204.1 us)
Async XLA Ops:
  7.2 141.7 %all-gather.10.cloned.1.call-start = ((), (), s32[]{:S(2)}) async-start(), calls=%async_computation.1 | async-start | bytes 17825792 | tf_op jit(solution)/shard_map/all_gather | solution.py:17
  7.9 97.6 %copy-start.13 = (f32[32]{0:T(128)}, f32[32]{0:T(128)S(1)}, u32[]{:S(2)}) copy-start(f32[32]{0:T(128)S(1)} %neg.50) | copy-start | bytes 388
  33.4 228.6 %all-gather.8.cloned.1.call-start = ((), (), s32[]{:S(2)}) async-start(), calls=%async_computation | async-start | bytes 17825792 | tf_op jit(solution)/shard_map/all_gather | solution.py:17
  43.2 3.3 copy-start.5
  46.6 58.9 %copy-start.7 = (f32[32,4,256]{2,1,0:T(4,128)}, f32[32,4,256]{2,1,0:T(4,128)S(1)}, u32[]{:S(2)}) copy-start(f32[32,4,256]{2,1,0:T(4,128)S(1)} %squeeze.124) | copy-start | bytes 393220
  54.6 12.9 %copy-start.16 = (u32[128]{0:T(128)S(1)}, u32[128]{0:T(128)}, u32[]{:S(2)}) copy-start(u32[128]{0:T(128)} %constant.194) | copy-start | bytes 1540
  54.6 50.9 %copy-start.10 = (f32[32]{0:T(128)S(1)}, f32[32]{0:T(128)}, u32[]{:S(2)}) copy-start(f32[32]{0:T(128)} %param.20) | copy-start | bytes 388
  327.6 8.2 %copy-start.3 = (f32[256,256]{1,0:T(8,128)}, f32[256,256]{1,0:T(8,128)S(1)}, u32[]{:S(2)}) copy-start(f32[256,256]{1,0:T(8,128)S(1)} %fusion.163) | copy-start | bytes 786436 | tf_op jit(solution)/shard_map/transpose(jvp())/while
  345.5 18.4 %copy-start.12 = (f32[32]{0:T(128)S(1)}, f32[32]{0:T(128)}, u32[]{:S(2)}) copy-start(f32[32]{0:T(128)} %fusion.168) | copy-start | bytes 388 | tf_op jit(solution)/shard_map/transpose(jvp())/while
  350.0 7.1 %copy-start.2 = (f32[1,32,256]{1,2,0:T(8,128)S(1)}, f32[1,32,256]{1,2,0:T(8,128)}, u32[]{:S(2)}) copy-start(f32[1,32,256]{1,2,0:T(8,128)} %get-tuple-element.1214) | copy-start | bytes 98308 | tf_op jit(solution)/shard_map/transpose(jvp())/while
  350.0 7.7 %copy-start.1 = (f32[32,256]{0,1:T(8,128)S(1)}, f32[32,256]{0,1:T(8,128)}, u32[]{:S(2)}) copy-start(f32[32,256]{0,1:T(8,128)} %get-tuple-element.1215) | copy-start | bytes 98308 | tf_op jit(solution)/shard_map/transpose(jvp())/while
  351.0 13.6 %copy-start.4 = (f32[32,256]{1,0:T(8,128)S(1)}, f32[32,256]{1,0:T(8,128)}, u32[]{:S(2)}) copy-start(f32[32,256]{1,0:T(8,128)} %copy_bitcast_fusion.10) | copy-start | bytes 98308 | tf_op jit(solution)/shard_map/transpose(jvp())/while
  351.0 13.6 %copy-start.15 = (f32[32]{0:T(128)S(1)}, f32[32]{0:T(128)}, u32[]{:S(2)}) copy-start(f32[32]{0:T(128)} %get-tuple-element.1211) | copy-start | bytes 388 | tf_op jit(solution)/shard_map/transpose(jvp())/while
  353.0 11.6 %copy-start = (bf16[256,32,64]{0,2,1:T(8,128)(2,1)S(1)}, bf16[256,32,64]{0,2,1:T(8,128)(2,1)}, u32[]{:S(2)}) copy-start(bf16[256,32,64]{0,2,1:T(8,128)(2,1)} %get-tuple-element.1210) | copy-start | bytes 3145732 | tf_op jit(solution)/shard_map/transpose(jvp())/while
  381.9 8.2 %copy-start.3 = (f32[256,256]{1,0:T(8,128)}, f32[256,256]{1,0:T(8,128)S(1)}, u32[]{:S(2)}) copy-start(f32[256,256]{1,0:T(8,128)S(1)} %fusion.163) | copy-start | bytes 786436 | tf_op jit(solution)/shard_map/transpose(jvp())/while
  399.8 18.4 %copy-start.12 = (f32[32]{0:T(128)S(1)}, f32[32]{0:T(128)}, u32[]{:S(2)}) copy-start(f32[32]{0:T(128)} %fusion.168) | copy-start | bytes 388 | tf_op jit(solution)/shard_map/transpose(jvp())/while
  404.2 7.1 %copy-start.2 = (f32[1,32,256]{1,2,0:T(8,128)S(1)}, f32[1,32,256]{1,2,0:T(8,128)}, u32[]{:S(2)}) copy-start(f32[1,32,256]{1,2,0:T(8,128)} %get-tuple-element.1214) | copy-start | bytes 98308 | tf_op jit(solution)/shard_map/transpose(jvp())/while
  404.2 7.7 %copy-start.1 = (f32[32,256]{0,1:T(8,128)S(1)}, f32[32,256]{0,1:T(8,128)}, u32[]{:S(2)}) copy-start(f32[32,256]{0,1:T(8,128)} %get-tuple-element.1215) | copy-start | bytes 98308 | tf_op jit(solution)/shard_map/transpose(jvp())/while
  405.2 13.6 %copy-start.4 = (f32[32,256]{1,0:T(8,128)S(1)}, f32[32,256]{1,0:T(8,128)}, u32[]{:S(2)}) copy-start(f32[32,256]{1,0:T(8,128)} %copy_bitcast_fusion.10) | copy-start | bytes 98308 | tf_op jit(solution)/shard_map/transpose(jvp())/while
  405.2 13.6 %copy-start.15 = (f32[32]{0:T(128)S(1)}, f32[32]{0:T(128)}, u32[]{:S(2)}) copy-start(f32[32]{0:T(128)} %get-tuple-element.1211) | copy-start | bytes 388 | tf_op jit(solution)/shard_map/transpose(jvp())/while
  407.2 11.6 %copy-start = (bf16[256,32,64]{0,2,1:T(8,128)(2,1)S(1)}, bf16[256,32,64]{0,2,1:T(8,128)(2,1)}, u32[]{:S(2)}) copy-start(bf16[256,32,64]{0,2,1:T(8,128)(2,1)} %get-tuple-element.1210) | copy-start | bytes 3145732 | tf_op jit(solution)/shard_map/transpose(jvp())/while
  436.1 8.2 %copy-start.3 = (f32[256,256]{1,0:T(8,128)}, f32[256,256]{1,0:T(8,128)S(1)}, u32[]{:S(2)}) copy-start(f32[256,256]{1,0:T(8,128)S(1)} %fusion.163) | copy-start | bytes 786436 | tf_op jit(solution)/shard_map/transpose(jvp())/while
  454.0 18.4 %copy-start.12 = (f32[32]{0:T(128)S(1)}, f32[32]{0:T(128)}, u32[]{:S(2)}) copy-start(f32[32]{0:T(128)} %fusion.168) | copy-start | bytes 388 | tf_op jit(solution)/shard_map/transpose(jvp())/while
  458.5 7.1 %copy-start.2 = (f32[1,32,256]{1,2,0:T(8,128)S(1)}, f32[1,32,256]{1,2,0:T(8,128)}, u32[]{:S(2)}) copy-start(f32[1,32,256]{1,2,0:T(8,128)} %get-tuple-element.1214) | copy-start | bytes 98308 | tf_op jit(solution)/shard_map/transpose(jvp())/while
  458.5 7.7 %copy-start.1 = (f32[32,256]{0,1:T(8,128)S(1)}, f32[32,256]{0,1:T(8,128)}, u32[]{:S(2)}) copy-start(f32[32,256]{0,1:T(8,128)} %get-tuple-element.1215) | copy-start | bytes 98308 | tf_op jit(solution)/shard_map/transpose(jvp())/while
  459.5 13.6 %copy-start.4 = (f32[32,256]{1,0:T(8,128)S(1)}, f32[32,256]{1,0:T(8,128)}, u32[]{:S(2)}) copy-start(f32[32,256]{1,0:T(8,128)} %copy_bitcast_fusion.10) | copy-start | bytes 98308 | tf_op jit(solution)/shard_map/transpose(jvp())/while
  459.5 13.6 %copy-start.15 = (f32[32]{0:T(128)S(1)}, f32[32]{0:T(128)}, u32[]{:S(2)}) copy-start(f32[32]{0:T(128)} %get-tuple-element.1211) | copy-start | bytes 388 | tf_op jit(solution)/shard_map/transpose(jvp())/while
  461.5 11.6 %copy-start = (bf16[256,32,64]{0,2,1:T(8,128)(2,1)S(1)}, bf16[256,32,64]{0,2,1:T(8,128)(2,1)}, u32[]{:S(2)}) copy-start(bf16[256,32,64]{0,2,1:T(8,128)(2,1)} %get-tuple-element.1210) | copy-start | bytes 3145732 | tf_op jit(solution)/shard_map/transpose(jvp())/while
  490.4 8.2 %copy-start.3 = (f32[256,256]{1,0:T(8,128)}, f32[256,256]{1,0:T(8,128)S(1)}, u32[]{:S(2)}) copy-start(f32[256,256]{1,0:T(8,128)S(1)} %fusion.163) | copy-start | bytes 786436 | tf_op jit(solution)/shard_map/transpose(jvp())/while
  508.2 18.4 %copy-start.12 = (f32[32]{0:T(128)S(1)}, f32[32]{0:T(128)}, u32[]{:S(2)}) copy-start(f32[32]{0:T(128)} %fusion.168) | copy-start | bytes 388 | tf_op jit(solution)/shard_map/transpose(jvp())/while
  512.7 7.1 %copy-start.2 = (f32[1,32,256]{1,2,0:T(8,128)S(1)}, f32[1,32,256]{1,2,0:T(8,128)}, u32[]{:S(2)}) copy-start(f32[1,32,256]{1,2,0:T(8,128)} %get-tuple-element.1214) | copy-start | bytes 98308 | tf_op jit(solution)/shard_map/transpose(jvp())/while
  512.7 7.7 %copy-start.1 = (f32[32,256]{0,1:T(8,128)S(1)}, f32[32,256]{0,1:T(8,128)}, u32[]{:S(2)}) copy-start(f32[32,256]{0,1:T(8,128)} %get-tuple-element.1215) | copy-start | bytes 98308 | tf_op jit(solution)/shard_map/transpose(jvp())/while
  513.7 13.6 %copy-start.4 = (f32[32,256]{1,0:T(8,128)S(1)}, f32[32,256]{1,0:T(8,128)}, u32[]{:S(2)}) copy-start(f32[32,256]{1,0:T(8,128)} %copy_bitcast_fusion.10) | copy-start | bytes 98308 | tf_op jit(solution)/shard_map/transpose(jvp())/while
  513.7 13.6 %copy-start.15 = (f32[32]{0:T(128)S(1)}, f32[32]{0:T(128)}, u32[]{:S(2)}) copy-start(f32[32]{0:T(128)} %get-tuple-element.1211) | copy-start | bytes 388 | tf_op jit(solution)/shard_map/transpose(jvp())/while
  515.7 11.6 %copy-start = (bf16[256,32,64]{0,2,1:T(8,128)(2,1)S(1)}, bf16[256,32,64]{0,2,1:T(8,128)(2,1)}, u32[]{:S(2)}) copy-start(bf16[256,32,64]{0,2,1:T(8,128)(2,1)} %get-tuple-element.1210) | copy-start | bytes 3145732 | tf_op jit(solution)/shard_map/transpose(jvp())/while
  585.5 12.4 %copy-start.6 = (f32[1,32,1024]{2,1,0:T(8,128)S(1)}, f32[1,32,1024]{2,1,0:T(8,128)}, u32[]{:S(2)}) copy-start(f32[1,32,1024]{2,1,0:T(8,128)} %param.19) | copy-start | bytes 393220
  585.5 12.4 %copy-start.11 = (f32[32]{0:T(128)S(1)}, f32[32]{0:T(128)}, u32[]{:S(2)}) copy-start(f32[32]{0:T(128)} %param.20) | copy-start | bytes 388
  585.5 12.4 %copy-start.14 = (f32[32]{0:T(128)S(1)}, f32[32]{0:T(128)}, u32[]{:S(2)}) copy-start(f32[32]{0:T(128)} %copy-done.13) | copy-start | bytes 388
  585.5 13.9 %copy-start.8 = (bf16[4,256,128]{2,1,0:T(8,128)(2,1)S(1)}, bf16[4,256,128]{2,1,0:T(8,128)(2,1)}, u32[]{:S(2)}) copy-start(bf16[4,256,128]{2,1,0:T(8,128)(2,1)} %get-tuple-element.600) | copy-start | bytes 786436
  585.5 13.8 %copy-start.9 = (bf16[4,256,128]{2,1,0:T(8,128)(2,1)S(1)}, bf16[4,256,128]{2,1,0:T(8,128)(2,1)}, u32[]{:S(2)}) copy-start(bf16[4,256,128]{2,1,0:T(8,128)(2,1)} %get-tuple-element.599) | copy-start | bytes 786436
Sparse Core Ops, SparseCore 0:
  33.5 115.2 all-gather.9
  151.0 110.9 all-gather.7
